TPU v7x, 32 devices: a whole 2x2x4 slice. The times are simulated.
32 devices in a mesh: row: 8 (over z, y), col: 4 (over x, core).
Axes of the slice: x: 2, y: 2, z: 4, core: 2. Of those that a mesh axis runs over, the one named last changes fastest.
Arguments:
- tile_u: bfloat16 [3, 8, 2, 4, 512, 128], P(None, 'row', None, 'col'), may hold values from -6 to 6
- tile_v: bfloat16 [3, 8, 2, 4, 512, 128], P(None, 'row', None, 'col'), may hold values from -6 to 6
- tile_ranks: int32 [3, 8, 2, 4], P(None, 'row', None, 'col'), may hold values from 16 to 128
- lower_inverse: bfloat16 [2, 512, 512], replicated, as said below
- upper_inverse: bfloat16 [2, 512, 512], replicated, as said below
- row_order: int32 [2, 512], replicated, may hold values from 0 to 511, each once within a row
- sketch: bfloat16 [512, 128], replicated, may hold values from -0.25 to 0.25
Outputs:
- new_u: bfloat16 [3, 8, 2, 4, 512, 128], P(None, 'row', None, 'col')
- new_v: bfloat16 [3, 8, 2, 4, 512, 128], P(None, 'row', None, 'col')
Inputs may be any that keep to these rules, and one draw needn't show every extreme that they name: Each row of row_order names every number of 0 to 511 once. Each lower_inverse[k] is lower triangular with a unit diagonal. Each upper_inverse[k] is upper triangular with a positive diagonal.
All inputs are finite; a program needn't handle non-finite values.
Results may differ from a plain program's by a relative error of at most 0.03.
Values may be sent and summed in bfloat16 or wider, within the bound.
A program may use at most 64 MiB of HBM per device.

v0:
```python
import jax
import jax.numpy as jnp
from jax import lax
from jax.sharding import PartitionSpec as P

PANELS = 2
HIGHEST = lax.Precision.HIGHEST


def from_root(array, axis, root):
    mine = lax.axis_index(axis) == root
    return lax.psum(jnp.where(mine, array, jnp.zeros_like(array)), axis)


def compress(tile_uf, tile_vf, left_u, coupling, top_v, keep_cols, sketch):
    rank_width = tile_uf.shape[-1]
    tile_size = tile_uf.shape[-2]
    product = jnp.einsum("...br,...rs->...bs", left_u, coupling, preferred_element_type=jnp.float32)
    update = (product * rank_width ** (-0.5)).astype(jnp.bfloat16)
    stacked_left = jnp.concatenate([tile_uf, -update], axis=-1)
    stacked_right = jnp.concatenate([tile_vf, top_v], axis=-1)
    probe_mat = jnp.einsum(
        "...bt,br->...tr", stacked_right, sketch, preferred_element_type=jnp.float32
    )
    left_wide = stacked_left.astype(jnp.float32)
    sample = (
        jnp.einsum("...bt,...tr->...br", left_wide, probe_mat, precision=HIGHEST)
        * keep_cols[..., None, :]
    )
    gram_matrix = jnp.einsum("...br,...bs->...rs", sample, sample, precision=HIGHEST)
    gram_matrix = gram_matrix + (1.0 - keep_cols)[..., :, None] * jnp.eye(
        rank_width, dtype=jnp.float32
    )
    factor = jnp.linalg.cholesky(gram_matrix)
    solved = lax.linalg.triangular_solve(
        factor, jnp.swapaxes(sample, -1, -2), left_side=True, lower=True
    )
    new_basis = jnp.swapaxes(solved, -1, -2)
    weights_q = jnp.einsum("...bt,...br->...tr", left_wide, new_basis, precision=HIGHEST)
    fresh_v = jnp.einsum(
        "...bt,...tr->...br", stacked_right.astype(jnp.float32), weights_q, precision=HIGHEST
    )
    return (
        (new_basis * tile_size**0.5).astype(jnp.bfloat16),
        (fresh_v * tile_size ** (-0.5)).astype(jnp.bfloat16),
    )


def on_device(tile_u, tile_v, tile_ranks, lower_inverse, upper_inverse, row_order, sketch):
    row_tiles, col_tiles = (tile_u.shape[0], tile_u.shape[2])
    tile_size, rank_width = (tile_u.shape[4], tile_u.shape[5])
    shape_four = (row_tiles, col_tiles, tile_size, rank_width)
    tile_rank = tile_ranks.reshape(row_tiles, col_tiles)
    keep_flags_mask = jnp.arange(rank_width, dtype=jnp.int32)[None, None, :] < tile_rank[:, :, None]
    keep_cols = keep_flags_mask.astype(jnp.float32)
    keep_half = keep_flags_mask.astype(jnp.bfloat16)[:, :, None, :]
    factor_left_bases = tile_u.reshape(shape_four) * keep_half
    factors_v = tile_v.reshape(shape_four) * keep_half
    row_place = lax.axis_index("row")
    col_place = lax.axis_index("col")
    global_rows = jnp.arange(row_tiles, dtype=jnp.int32) * lax.axis_size("row") + row_place
    global_cols = jnp.arange(col_tiles, dtype=jnp.int32) * lax.axis_size("col") + col_place

    def prepare(panel, factor_left_bases, factors_v):
        permuted = jnp.take(factor_left_bases[0], row_order[panel], axis=1)
        turned_u = jnp.einsum(
            "ab,mbr->mar", lower_inverse[panel], permuted, preferred_element_type=jnp.float32
        ).astype(jnp.bfloat16)
        top_u = jnp.where((global_cols > panel)[:, None, None], turned_u, factor_left_bases[0])
        transposed_right_basis = jnp.einsum(
            "ba,lbr->lar", upper_inverse[panel], factors_v[:, 0], preferred_element_type=jnp.float32
        )
        transposed_right_basis = (transposed_right_basis * tile_size**0.5).astype(jnp.bfloat16)
        left_right_basis = jnp.where(
            (global_rows > panel)[:, None, None], transposed_right_basis, factors_v[:, 0]
        )
        factor_left_bases = factor_left_bases.at[0].set(
            jnp.where(row_place == panel, top_u, factor_left_bases[0])
        )
        factors_v = factors_v.at[:, 0].set(
            jnp.where(col_place == panel, left_right_basis, factors_v[:, 0])
        )
        panel_upper_left_basis, panel_top_v = (
            from_root(top_u, "row", panel),
            from_root(factors_v[0], "row", panel),
        )
        panel_left_u, panel_left_right_basis = (
            from_root(factor_left_bases[:, 0], "col", panel),
            from_root(left_right_basis, "col", panel),
        )
        coupling = jnp.einsum(
            "nxu,ixp->niup",
            panel_left_right_basis,
            panel_upper_left_basis,
            preferred_element_type=jnp.float32,
        )
        coupling = (coupling * tile_size ** (-0.5)).astype(jnp.bfloat16)
        return (factor_left_bases, factors_v, panel_left_u, coupling, panel_top_v)

    def refresh(
        panel, block_u, block_v, left_u, coupling, top_v, keep_block, rows_block, cols_block
    ):
        left_full = jnp.broadcast_to(left_u[:, None], block_u.shape)
        top_full = jnp.broadcast_to(top_v[None, :], block_v.shape)
        fresh_u, fresh_v = compress(
            block_u, block_v, left_full, coupling, top_full, keep_block, sketch
        )
        chosen = ((rows_block > panel)[:, None] & (cols_block > panel)[None, :])[:, :, None, None]
        return (jnp.where(chosen, fresh_u, block_u), jnp.where(chosen, fresh_v, block_v))

    prepared = prepare(0, factor_left_bases, factors_v)
    for panel in range(PANELS):
        factor_left_bases, factors_v, left_u, coupling, top_v = prepared
        if panel + 1 < PANELS:
            head_u, head_v = refresh(
                panel,
                factor_left_bases[:1],
                factors_v[:1],
                left_u[:1],
                coupling[:1],
                top_v,
                keep_cols[:1],
                global_rows[:1],
                global_cols,
            )
            lateral_left_basis, side_v = refresh(
                panel,
                factor_left_bases[1:, :1],
                factors_v[1:, :1],
                left_u[1:],
                coupling[1:, :1],
                top_v[:1],
                keep_cols[1:, :1],
                global_rows[1:],
                global_cols[:1],
            )
            factor_left_bases = (
                factor_left_bases.at[:1].set(head_u).at[1:, :1].set(lateral_left_basis)
            )
            factors_v = factors_v.at[:1].set(head_v).at[1:, :1].set(side_v)
            prepared = prepare(panel + 1, factor_left_bases, factors_v)
            factor_left_bases, factors_v = (prepared[0], prepared[1])
            inner_u, inner_v = refresh(
                panel,
                factor_left_bases[1:, 1:],
                factors_v[1:, 1:],
                left_u[1:],
                coupling[1:, 1:],
                top_v[1:],
                keep_cols[1:, 1:],
                global_rows[1:],
                global_cols[1:],
            )
            factor_left_bases = factor_left_bases.at[1:, 1:].set(inner_u)
            factors_v = factors_v.at[1:, 1:].set(inner_v)
            prepared = (factor_left_bases, factors_v) + tuple(prepared[2:])
        else:
            factor_left_bases, factors_v = refresh(
                panel,
                factor_left_bases,
                factors_v,
                left_u,
                coupling,
                top_v,
                keep_cols,
                global_rows,
                global_cols,
            )
    return (factor_left_bases.reshape(tile_u.shape), factors_v.reshape(tile_v.shape))


def solution(mesh):
    in_specs = (
        P(None, "row", None, "col", None, None),
        P(None, "row", None, "col", None, None),
        P(None, "row", None, "col"),
        P(),
        P(),
        P(),
        P(),
    )
    out_specs = (P(None, "row", None, "col", None, None), P(None, "row", None, "col", None, None))
    return jax.shard_map(
        on_device, mesh=mesh, in_specs=in_specs, out_specs=out_specs, check_vma=False
    )
```

profile of v0, /device:TPU:0, one launch (start us, length us, event | category | flops | bytes accessed | tf_op | source)
XLA Modules:
  0.0 551.3 jit_solution(12464353481008873408)
XLA Ops:
  7.2 1.5 copy.185
  8.8 0.7 fusion.117
  11.5 2.1 gather_fusion
  13.6 1.8 fusion.90
  15.4 2.2 broadcast_select_fusion.6
  17.6 0.8 fusion.65
  18.4 1.1 broadcast_select_fusion.4
  19.7 0.8 select_bitcast_fusion.1
  20.7 0.7 slice_bitcast_fusion.5
  21.5 0.7 slice_bitcast_fusion.7
  23.4 0.7 broadcast_subtract_fusion
  24.8 0.7 fusion.136
  26.7 0.7 compare_and_fusion.2
  28.5 0.7 slice_bitcast_fusion.8
  29.3 28.2 %all-reduce.15.cloned.1.call-done = (bf16[3,512,128]{1,2,0:T(8,128)(2,1)}, bf16[3,512,128]{1,2,0:T(8,128)(2,1)}) async-done(((bf16[3,512,128]{1,2,0:T(8,128)(2,1)}, bf16[3,512,128]{1,2,0:T(8,128)(2,1)}), (bf16[3,512,128]{1,2,0:T(8,128)(2,1)}, bf16[3,512,128]{1,2,0:T(8,128)(2,1)})) %all-reduce.15.cloned.1.call-update) | async-done | bytes 786448 | tf_op jit(solution)/shard_map/psum | solution.py:12
  57.5 1.0 slice_bitcast_fusion.11
  58.6 75.1 %all-reduce.11.cloned.1.call-done = (bf16[2,512,128]{1,2,0:T(8,128)(2,1)}, bf16[2,512,128]{1,2,0:T(8,128)(2,1)}) async-done(((bf16[2,512,128]{1,2,0:T(8,128)(2,1)}, bf16[2,512,128]{1,2,0:T(8,128)(2,1)}), (bf16[2,512,128]{1,2,0:T(8,128)(2,1)}, bf16[2,512,128]{1,2,0:T(8,128)(2,1)})) %all-reduce.11.cloned.1.call-update) | async-done | bytes 524304 | tf_op jit(solution)/shard_map/psum | solution.py:12
  133.7 1.5 fusion.34
  135.2 1.9 fusion.21
  137.6 0.7 slice_bitcast_fusion.9
  138.6 0.7 convolution_multiply_fusion.11
  139.3 1.0 fusion.35
  140.5 23.6 %custom-call.20 = f32[1,2,128,128]{3,2,1,0:T(8,128)S(1)} custom-call(f32[1,2,128,128]{3,2,1,0:T(8,128)S(1)} %copy.193), custom_call_target="Cholesky" | custom-call | tf_op jit(solution)/shard_map/jit(cholesky)/cholesky | solution.py:34
  164.4 20.3 %custom-call.21 = f32[1,2,1,128,128]{3,4,2,1,0:T(8,128)} custom-call(f32[1,2,1,128,128]{4,3,2,1,0:T(8,128)S(1)} %select_bitcast_fusion.3), custom_call_target="InvertDiagBlocksLowerTriangular" | custom-call | tf_op jit(solution)/shard_map/triangular_solve | solution.py:35
  184.7 0.9 broadcast_in_dim.170
  185.7 1.3 fusion.62
  187.0 1.7 convolution_multiply_fusion.10
  188.7 2.5 convolution_add_fusion.1
  191.2 1.6 copy.201
  192.9 1.6 fusion.98
  194.5 24.9 %custom-call.26 = f32[2,1,128,128]{3,2,1,0:T(8,128)} custom-call(f32[2,1,128,128]{3,2,1,0:T(8,128)} %fusion.98), custom_call_target="Cholesky" | custom-call | tf_op jit(solution)/shard_map/jit(cholesky)/cholesky | solution.py:34
  219.4 0.9 fusion.105
  220.5 1.6 fusion.108
  222.1 21.3 %custom-call.27 = f32[2,1,1,128,128]{3,4,2,1,0:T(8,128)} custom-call(f32[2,1,1,128,128]{4,3,2,1,0:T(8,128)} %fusion.108), custom_call_target="InvertDiagBlocksLowerTriangular" | custom-call | tf_op jit(solution)/shard_map/triangular_solve/custom-call.4 | solution.py:35
  243.4 2.4 fusion.78
  245.8 1.5 fusion.81
  247.5 2.1 gather_fusion.1
  249.6 1.8 fusion.91
  251.4 2.1 broadcast_select_fusion.5
  253.7 0.8 fusion.64
  257.0 0.7 copy-done.60
  257.7 1.2 bitcast_dynamic-update-slice_fusion
  259.7 0.7 convolution_multiply_fusion.7
  260.4 1.0 convolution_add_fusion
  261.5 0.7 fusion.96
  262.2 24.3 %custom-call.28 = f32[2,1,128,128]{3,2,1,0:T(8,128)S(1)} custom-call(f32[2,1,128,128]{3,2,1,0:T(8,128)} %fusion.96), custom_call_target="Cholesky" | custom-call | tf_op jit(solution)/shard_map/jit(cholesky)/cholesky | solution.py:34
  286.6 0.8 broadcast_select_fusion.2
  287.6 20.1 %custom-call.29 = f32[2,1,1,128,128]{3,4,2,1,0:T(8,128)S(1)} custom-call(f32[2,1,1,128,128]{4,3,2,1,0:T(8,128)S(1)} %fusion.103), custom_call_target="InvertDiagBlocksLowerTriangular" | custom-call | tf_op jit(solution)/shard_map/triangular_solve/custom-call.4 | solution.py:35
  307.7 0.7 fusion.85
  308.4 1.4 fusion.84
  310.9 11.1 %all-reduce.13.cloned.1.call-done = (bf16[3,512,128]{1,2,0:T(8,128)(2,1)}, bf16[3,512,128]{1,2,0:T(8,128)(2,1)}) async-done(((bf16[3,512,128]{1,2,0:T(8,128)(2,1)}, bf16[3,512,128]{1,2,0:T(8,128)(2,1)}), (bf16[3,512,128]{1,2,0:T(8,128)(2,1)}, bf16[3,512,128]{1,2,0:T(8,128)(2,1)})) %all-reduce.13.cloned.1.call-update) | async-done | bytes 786448 | tf_op jit(solution)/shard_map/psum | solution.py:12
  322.0 1.2 copy.225
  323.2 74.9 %all-reduce.9.cloned.1.call-done = (bf16[2,512,128]{1,2,0:T(8,128)(2,1)}, bf16[2,512,128]{1,2,0:T(8,128)(2,1)}) async-done(((bf16[2,512,128]{1,2,0:T(8,128)(2,1)}, bf16[2,512,128]{1,2,0:T(8,128)(2,1)}), (bf16[2,512,128]{1,2,0:T(8,128)(2,1)}, bf16[2,512,128]{1,2,0:T(8,128)(2,1)})) %all-reduce.9.cloned.1.call-update) | async-done | bytes 524304 | tf_op jit(solution)/shard_map/psum | solution.py:12
  398.1 1.0 broadcast_in_dim.178
  401.2 1.6 convolution_multiply_fusion
  402.8 2.6 fusion.137
  405.7 1.0 fusion.69
  406.6 71.3 %custom-call.22 = f32[3,2,128,128]{3,2,1,0:T(8,128)S(1)} custom-call(f32[3,2,128,128]{3,2,1,0:T(8,128)} %fusion.69), custom_call_target="Cholesky" | custom-call | tf_op jit(solution)/shard_map/jit(cholesky)/cholesky | solution.py:34
  478.3 59.0 %custom-call.23 = f32[3,2,1,128,128]{3,4,2,1,0:T(8,128)S(1)} custom-call(f32[3,2,1,128,128]{4,3,2,1,0:T(8,128)S(1)} %select_bitcast_fusion), custom_call_target="InvertDiagBlocksLowerTriangular" | custom-call | tf_op jit(solution)/shard_map/triangular_solve | solution.py:35
  537.3 1.5 fusion.66
  538.8 1.4 fusion.41
  540.7 1.2 copy.238
  542.3 1.1 fusion.5
  543.4 1.2 copy.239
  (199 shorter events, 15.2 us)
Async XLA Ops:
  7.2 131.1 %copy-start = (bf16[512,128]{1,0:T(8,128)(2,1)S(1)}, bf16[512,128]{1,0:T(8,128)(2,1)}, u32[]{:S(2)}) copy-start(bf16[512,128]{1,0:T(8,128)(2,1)} %param.38) | copy-start | bytes 393220
  7.2 1.6 copy-start.55
  7.2 2.3 copy-start.16
  7.2 50.3 %all-reduce.15.cloned.1.call-start = ((), (), s32[]{:S(2)}) async-start(), calls=%async_computation.3 | async-start | bytes 1572864 | tf_op jit(solution)/shard_map/psum | solution.py:12
  8.8 1.1 copy-start.44
  15.3 3.1 copy-start.59
  19.5 1.9 copy-start.11
  19.6 114.2 %all-reduce.11.cloned.1.call-start = ((), (), s32[]{:S(2)}) async-start(), calls=%async_computation.1 | async-start | bytes 1048576 | tf_op jit(solution)/shard_map/psum | solution.py:12
  19.7 1.7 copy-start.1
  20.5 1.7 copy-start.42
  20.5 3.0 copy-start.45
  20.5 301.5 %all-reduce.13.cloned.1.call-start = ((), (), s32[]{:S(2)}) async-start(), calls=%async_computation.2 | async-start | bytes 1572864 | tf_op jit(solution)/shard_map/psum | solution.py:12
  21.4 115.7 %copy-start.19 = (f32[128,128]{1,0:T(8,128)}, f32[128,128]{1,0:T(8,128)S(1)}, u32[]{:S(2)}) copy-start(f32[128,128]{1,0:T(8,128)S(1)} %fusion.116) | copy-start | bytes 196612
  21.4 142.7 %copy-start.22 = (pred[128,128]{1,0:T(8,128)(4,1)}, pred[128,128]{1,0:T(8,128)(4,1)S(1)}, u32[]{:S(2)}) copy-start(pred[128,128]{1,0:T(8,128)(4,1)S(1)} %iota_compare_fusion.1) | copy-start | bytes 49156
  22.8 114.5 %copy-start.61 = (pred[3]{0:T(512)(128)(4,1)}, pred[3]{0:T(512)(128)(4,1)S(1)}, u32[]{:S(2)}) copy-start(pred[3]{0:T(512)(128)(4,1)S(1)} %broadcast_compare_fusion.3) | copy-start | bytes 13
  24.7 112.6 %copy-start.56 = (pred[2]{0:T(512)(128)(4,1)}, pred[2]{0:T(512)(128)(4,1)S(1)}, u32[]{:S(2)}) copy-start(pred[2]{0:T(512)(128)(4,1)S(1)} %get-tuple-element.176) | copy-start | bytes 10
  24.8 160.9 %copy-start.14 = (f32[128,128]{0,1:T(8,128)}, f32[128,128]{0,1:T(8,128)S(1)}, u32[]{:S(2)}) copy-start(f32[128,128]{0,1:T(8,128)S(1)} %copy.190) | copy-start | bytes 196612
  57.5 79.6 %copy-start.13 = (bf16[3,512,128]{1,2,0:T(8,128)(2,1)S(1)}, bf16[3,512,128]{1,2,0:T(8,128)(2,1)}, u32[]{:S(2)}) copy-start(bf16[3,512,128]{1,2,0:T(8,128)(2,1)} %get-tuple-element.139) | copy-start | bytes 1179652
  133.7 3.8 copy-start.32
  133.7 4.5 copy-start.35
  185.6 1.3 copy-start.28
  243.4 2.4 copy-start.40
  243.4 2.4 copy-start.51
  245.8 1.7 copy-start.46
  245.8 3.8 copy-start.54
  247.3 4.1 copy-start.57
  251.4 3.1 copy-start.10
  253.6 1.6 copy-start.2
  253.6 1.6 copy-start.33
  253.6 1.6 copy-start.36
  253.6 1.6 copy-start.53
  254.5 1.1 copy-start.5
  254.5 1.2 copy-start.6
  254.5 1.3 copy-start.9
  255.2 1.2 copy-start.12
  255.2 1.2 copy-start.29
  255.2 1.2 copy-start.34
  255.2 1.2 copy-start.52
  256.5 1.2 copy-start.60
  256.5 1.2 copy-start.62
  257.7 1.2 copy-start.21
  258.9 0.8 copy-start.49
  258.9 1.5 copy-start.15
  258.9 1.6 copy-start.48
  259.7 26.8 %copy-start.23 = (pred[128,128]{1,0:T(8,128)(4,1)S(1)}, pred[128,128]{1,0:T(8,128)(4,1)}, u32[]{:S(2)}) copy-start(pred[128,128]{1,0:T(8,128)(4,1)} %copy-done.22) | copy-start | bytes 49156
  259.7 26.9 %copy-start.26 = (bf16[3,512,128]{1,2,0:T(8,128)(2,1)S(1)}, bf16[3,512,128]{1,2,0:T(8,128)(2,1)}, u32[]{:S(2)}) copy-start(bf16[3,512,128]{1,2,0:T(8,128)(2,1)} %get-tuple-element.170) | copy-start | bytes 1179652
  287.4 110.7 %all-reduce.9.cloned.1.call-start = ((), (), s32[]{:S(2)}) async-start(), calls=%async_computation | async-start | bytes 1048576 | tf_op jit(solution)/shard_map/psum | solution.py:12
  308.4 2.1 copy-start.31
  308.4 2.1 copy-start.38
  308.4 2.1 copy-start.50
  310.9 88.8 %copy-start.7 = (bf16[3,2,512,128]{2,3,1,0:T(8,128)(2,1)}, bf16[3,2,512,128]{2,3,1,0:T(8,128)(2,1)S(1)}, u32[]{:S(2)}) copy-start(bf16[3,2,512,128]{2,3,1,0:T(8,128)(2,1)S(1)} %fusion.40) | copy-start | bytes 2359300
  399.1 0.9 copy-start.17
  399.1 1.3 copy-start.25
  399.1 1.3 copy-start.39
  400.1 1.1 copy-start.43
  401.2 1.6 copy-start.3
  402.8 2.9 copy-start.20
  402.8 2.9 copy-start.27
  402.8 2.9 copy-start.41
  405.5 72.5 %copy-start.24 = (pred[128,128]{1,0:T(8,128)(4,1)S(1)}, pred[128,128]{1,0:T(8,128)(4,1)}, u32[]{:S(2)}) copy-start(pred[128,128]{1,0:T(8,128)(4,1)} %copy-done.22) | copy-start | bytes 49156
  537.3 1.5 copy-start.4
  538.8 1.4 copy-start.58
  540.7 1.2 copy-start.8
  540.7 1.6 copy-start.18
  (3 other events, 2.2 us)
Sparse Core Ops, SparseCore 0:
  19.7 37.7 all-reduce.14
  61.0 72.7 all-reduce.10
  287.6 34.3 all-reduce.12
  325.3 72.7 all-reduce.8
where the time goes:
time: 557 us; the launch traced here: 551 us
  other arithmetic  285 us (51%)
  waiting for transfers between devices  189 us (34%)
  matrix products  37.8 us (7%)
  local copies, waits for them, and re-layouts  22.4 us (4%)
  between operations  16.4 us (3%)
    psum x4, waiting for transfers between devices, from_root(): return lax.psum(jnp.where(mine, array, jnp.zeros_like(array)), axis)  189 us
    another operation x13, other arithmetic, compress(): factor = jnp.linalg.cholesky(gram_matrix)  146 us
    another operation x9, other arithmetic, compress(): lax.linalg.triangular_solve(factor, jnp.swapaxes(sample, -1, -2), left_si...  123 us
  transfers between devices with their start and end apart: 4, of which 4 were waited for; matrix products, arithmetic and copies ran while one was open for 6% of the time, Pallas kernels for 0%

commit v1 on v0

--- a/solution.py
+++ b/solution.py
@@ -7,9 +7,15 @@
 HIGHEST = lax.Precision.HIGHEST
 
 
+def gather_and_add(x, axis):
+    parts = lax.all_gather(x, axis, axis=0, tiled=False)
+    acc = parts.sum(axis=0)
+    return acc
+
+
 def from_root(array, axis, root):
     mine = lax.axis_index(axis) == root
-    return lax.psum(jnp.where(mine, array, jnp.zeros_like(array)), axis)
+    return gather_and_add(jnp.where(mine, array, jnp.zeros_like(array)), axis)
 
 
 def compress(tile_uf, tile_vf, left_u, coupling, top_v, keep_cols, sketch):

time: 557 us -> 577 us (1.036)
  other arithmetic: 285 us -> 296 us
  local copies, waits for them, and re-layouts: 22.4 us -> 29 us
  waiting for transfers between devices: 189 us -> 195 us
    all_gather x0 -> x8, waiting for transfers between devices: none -> 195 us  [gather_and_add(): parts = lax.all_gather(x, axis, axis=0, tiled=False)]
    psum x4 -> x0, waiting for transfers between devices: 189 us -> none  [from_root(): return lax.psum(jnp.where(mine, array, jnp.zeros_like(array)), axis)]
    reduce_sum x0 -> x8, other arithmetic: none -> 14.9 us  [gather_and_add(): acc = parts.sum(axis=0)]
    select_n x0 -> x8, local copies, waits for them, and re-layouts: none -> 7.24 us  [from_root(): return gather_and_add(jnp.where(mine, array, jnp.zeros_like(array)), axis)]
  transfers between devices with their start and end apart: 4 -> 8, of which waited for: 4 -> 6; matrix products, arithmetic and copies ran while one was open for 6% -> 16% of each run, Pallas kernels for 0% -> 0%
where the time goes in v1:
time: 577 us; the launch traced here: 570 us
  other arithmetic  296 us (51%)
  waiting for transfers between devices  195 us (34%)
  matrix products  32.6 us (6%)
  local copies, waits for them, and re-layouts  29 us (5%)
  between operations  17.1 us (3%)
    all_gather x8, waiting for transfers between devices, gather_and_add(): parts = lax.all_gather(x, axis, axis=0, tiled=False)  195 us
    another operation x13, other arithmetic, compress(): factor = jnp.linalg.cholesky(gram_matrix)  146 us
    another operation x9, other arithmetic, compress(): lax.linalg.triangular_solve(factor, jnp.swapaxes(sample, -1, -2), left_si...  121 us
    reduce_sum x8, other arithmetic, gather_and_add(): acc = parts.sum(axis=0)  14.9 us
  transfers between devices with their start and end apart: 8, of which 6 were waited for; matrix products, arithmetic and copies ran while one was open for 16% of the time, Pallas kernels for 0%

profile of v1, /device:TPU:0, one launch (start us, length us, event | category | flops | bytes accessed | tf_op | source)
XLA Modules:
  0.0 570.0 jit_solution(8653391741267884730)
XLA Ops:
  7.8 0.8 copy.335
  9.2 1.4 copy.334
  11.1 1.0 copy-done.50
  12.5 0.9 copy.345
  14.7 2.1 gather_fusion
  17.9 1.7 fusion.87
  19.6 1.4 broadcast_select_fusion.7
  21.1 0.9 copy.340
  22.2 0.9 copy.350
  23.2 0.9 copy.343
  32.8 3.2 all-gather.23.cloned.1.call-done
  36.0 1.7 reduce_sum.98
  37.7 20.1 %all-gather.19.cloned.1.call-done = bf16[12,1,512,128]{3,2,1,0:T(8,128)(2,1)} async-done(((bf16[3,1,512,128]{3,2,1,0:T(8,128)(2,1)}), bf16[12,1,512,128]{3,2,1,0:T(8,128)(2,1)}) %all-gather.19.cloned.1.call-update) | async-done | bytes 1572880 | tf_op jit(solution)/shard_map/all_gather | solution.py:11
  57.8 1.6 bitcast_reduce_fusion.1
  59.4 49.6 %all-gather.15.cloned.1.call-done = bf16[8,2,512,128]{3,2,1,0:T(8,128)(2,1)} async-done(((bf16[1,2,512,128]{3,2,1,0:T(8,128)(2,1)}), bf16[8,2,512,128]{3,2,1,0:T(8,128)(2,1)}) %all-gather.15.cloned.1.call-update) | async-done | bytes 2097168 | tf_op jit(solution)/shard_map/all_gather | solution.py:11
  109.0 2.0 reduce_sum.99
  111.0 0.9 copy.351
  112.5 46.1 %all-gather.21.cloned.1.call-done = bf16[16,512,128]{2,1,0:T(8,128)(2,1)} async-done(((bf16[2,512,128]{2,1,0:T(8,128)(2,1)}), bf16[16,512,128]{2,1,0:T(8,128)(2,1)}) %all-gather.21.cloned.1.call-update) | async-done | bytes 2097168 | tf_op jit(solution)/shard_map/all_gather | solution.py:11
  158.7 2.0 reduce_sum.97
  160.6 0.8 copy.362
  161.7 1.0 fusion.21
  163.0 1.4 fusion.63
  165.1 1.0 fusion.35
  166.2 0.8 copy.356
  166.9 0.9 fusion.105
  167.9 23.6 %custom-call.20 = f32[1,2,128,128]{3,2,1,0:T(8,128)S(1)} custom-call(f32[1,2,128,128]{3,2,1,0:T(8,128)S(1)} %copy.357), custom_call_target="Cholesky" | custom-call | tf_op jit(solution)/shard_map/jit(cholesky)/cholesky | solution.py:40
  191.6 0.8 select_reduce_fusion.1
  192.5 20.3 %custom-call.21 = f32[1,2,1,128,128]{3,4,2,1,0:T(8,128)} custom-call(f32[1,2,1,128,128]{4,3,2,1,0:T(8,128)S(1)} %select_bitcast_fusion.2), custom_call_target="InvertDiagBlocksLowerTriangular" | custom-call | tf_op jit(solution)/shard_map/triangular_solve | solution.py:41
  212.9 1.3 fusion.62
  214.2 1.7 convolution_multiply_fusion.10
  215.9 1.8 convolution_add_fusion.1
  218.5 1.6 fusion.93
  220.1 24.3 %custom-call.26 = f32[2,1,128,128]{3,2,1,0:T(8,128)S(1)} custom-call(f32[2,1,128,128]{3,2,1,0:T(8,128)} %fusion.93), custom_call_target="Cholesky" | custom-call | tf_op jit(solution)/shard_map/jit(cholesky)/cholesky | solution.py:40
  244.4 0.8 fusion.100
  246.0 20.7 %custom-call.27 = f32[2,1,1,128,128]{3,4,2,1,0:T(8,128)S(1)} custom-call(f32[2,1,1,128,128]{4,3,2,1,0:T(8,128)} %fusion.103), custom_call_target="InvertDiagBlocksLowerTriangular" | custom-call | tf_op jit(solution)/shard_map/triangular_solve/custom-call.4 | solution.py:41
  266.7 1.7 fusion.76
  272.7 1.0 copy.395
  274.0 2.1 gather_fusion.1
  276.1 1.8 fusion.88
  277.9 1.4 broadcast_select_fusion.5
  279.4 0.9 copy.390
  280.4 0.9 copy.393
  281.4 0.9 copy.401
  283.8 1.1 fusion.19
  285.6 1.4 convolution_multiply_fusion.7
  287.1 1.0 convolution_add_fusion
  288.2 23.9 %custom-call.28 = f32[2,1,128,128]{3,2,1,0:T(8,128)S(1)} custom-call(f32[2,1,128,128]{3,2,1,0:T(8,128)S(1)} %fusion.91), custom_call_target="Cholesky" | custom-call | tf_op jit(solution)/shard_map/jit(cholesky)/cholesky | solution.py:40
  312.3 19.8 %custom-call.29 = f32[2,1,1,128,128]{3,4,2,1,0:T(8,128)S(1)} custom-call(f32[2,1,1,128,128]{4,3,2,1,0:T(8,128)S(1)} %fusion.98), custom_call_target="InvertDiagBlocksLowerTriangular" | custom-call | tf_op jit(solution)/shard_map/triangular_solve/custom-call.4 | solution.py:41
  334.0 2.0 reduce_sum.102
  336.1 1.6 bitcast_reduce_fusion
  337.7 27.7 %all-gather.27.cloned.1.call-done = bf16[16,512,128]{2,1,0:T(8,128)(2,1)} async-done(((bf16[2,512,128]{2,1,0:T(8,128)(2,1)}), bf16[16,512,128]{2,1,0:T(8,128)(2,1)}) %all-gather.27.cloned.1.call-update) | async-done | bytes 2097168 | tf_op jit(solution)/shard_map/all_gather | solution.py:11
  365.4 2.0 reduce_sum.101
  367.3 47.8 %all-gather.17.cloned.1.call-done = bf16[8,2,512,128]{3,2,1,0:T(8,128)(2,1)} async-done(((bf16[1,2,512,128]{3,2,1,0:T(8,128)(2,1)}), bf16[8,2,512,128]{3,2,1,0:T(8,128)(2,1)}) %all-gather.17.cloned.1.call-update) | async-done | bytes 2097168 | tf_op jit(solution)/shard_map/all_gather | solution.py:11
  415.1 2.0 reduce_sum.103
  419.1 1.6 convolution_multiply_fusion
  420.7 2.6 fusion.132
  423.6 0.9 fusion.69
  424.5 71.3 %custom-call.22 = f32[3,2,128,128]{3,2,1,0:T(8,128)S(1)} custom-call(f32[3,2,128,128]{3,2,1,0:T(8,128)} %fusion.69), custom_call_target="Cholesky" | custom-call | tf_op jit(solution)/shard_map/jit(cholesky)/cholesky | solution.py:40
  496.2 59.0 %custom-call.23 = f32[3,2,1,128,128]{3,4,2,1,0:T(8,128)S(1)} custom-call(f32[3,2,1,128,128]{4,3,2,1,0:T(8,128)S(1)} %select_bitcast_fusion), custom_call_target="InvertDiagBlocksLowerTriangular" | custom-call | tf_op jit(solution)/shard_map/triangular_solve | solution.py:41
  555.2 1.5 fusion.66
  556.7 1.4 fusion.41
  559.5 1.1 fusion.5
  560.7 1.2 copy.412
  561.8 1.2 copy.411
  (209 shorter events, 28.5 us)
Async XLA Ops:
  7.2 155.8 %copy-start = (bf16[512,128]{1,0:T(8,128)(2,1)S(1)}, bf16[512,128]{1,0:T(8,128)(2,1)}, u32[]{:S(2)}) copy-start(bf16[512,128]{1,0:T(8,128)(2,1)} %param.38) | copy-start | bytes 393220
  7.2 3.4 copy-start.16
  7.2 28.8 %all-gather.23.cloned.1.call-start = ((), (), s32[]{:S(2)}) async-start(), calls=%async_computation.4 | async-start | bytes 1966080 | tf_op jit(solution)/shard_map/all_gather | solution.py:11
  8.5 2.3 copy-start.38
  10.9 1.2 copy-start.50
  12.5 9.6 %copy-start.11 = (bf16[3,512,128]{1,2,0:T(8,128)(2,1)}, bf16[3,512,128]{1,2,0:T(8,128)(2,1)S(1)}, u32[]{:S(2)}) copy-start(bf16[3,512,128]{1,2,0:T(8,128)(2,1)S(1)} %get-tuple-element.140) | copy-start | bytes 1179652
  13.4 0.7 copy-start.41
  13.5 44.3 %all-gather.19.cloned.1.call-start = ((), (), s32[]{:S(2)}) async-start(), calls=%async_computation.2 | async-start | bytes 1966080 | tf_op jit(solution)/shard_map/all_gather | solution.py:11
  22.1 87.0 %all-gather.15.cloned.1.call-start = ((), (), s32[]{:S(2)}) async-start(), calls=%async_computation | async-start | bytes 2359296 | tf_op jit(solution)/shard_map/all_gather | solution.py:11
  22.2 8.4 %copy-start.1 = (bf16[3,2,512,128]{2,3,0,1:T(8,128)(2,1)}, bf16[3,2,512,128]{2,3,0,1:T(8,128)(2,1)S(1)}, u32[]{:S(2)}) copy-start(bf16[3,2,512,128]{2,3,0,1:T(8,128)(2,1)S(1)} %bitcast_dynamic-update-slice_fusion.1) | copy-start | bytes 2359300
  23.1 6.4 %copy-start.36 = (f32[3,2,128]{2,1,0:T(2,128)S(1)}, f32[3,2,128]{2,1,0:T(2,128)}, u32[]{:S(2)}) copy-start(f32[3,2,128]{2,1,0:T(2,128)} %get-tuple-element.151) | copy-start | bytes 9220
  23.1 135.5 %all-gather.21.cloned.1.call-start = ((), (), s32[]{:S(2)}) async-start(), calls=%async_computation.3 | async-start | bytes 2359296 | tf_op jit(solution)/shard_map/all_gather | solution.py:11
  23.2 8.1 %copy-start.12 = (bf16[3,512,128]{1,2,0:T(8,128)(2,1)S(1)}, bf16[3,512,128]{1,2,0:T(8,128)(2,1)}, u32[]{:S(2)}) copy-start(bf16[3,512,128]{1,2,0:T(8,128)(2,1)} %copy-done.11) | copy-start | bytes 1179652
  24.1 309.9 %all-gather.29.cloned.1.call-start = ((), (), s32[]{:S(2)}) async-start(), calls=%async_computation.7 | async-start | bytes 1966080 | tf_op jit(solution)/shard_map/all_gather | solution.py:11
  26.9 10.8 %copy-start.20 = (f32[128,128]{1,0:T(8,128)}, f32[128,128]{1,0:T(8,128)S(1)}, u32[]{:S(2)}) copy-start(f32[128,128]{1,0:T(8,128)S(1)} %get-tuple-element.180) | copy-start | bytes 196612
  161.4 3.0 copy-start.43
  161.7 3.4 copy-start.19
  162.7 2.4 copy-start.14
  162.7 2.4 copy-start.42
  163.0 3.2 copy-start.5
  165.1 47.7 %copy-start.22 = (bf16[512,128]{0,1:T(8,128)(2,1)S(1)}, bf16[512,128]{0,1:T(8,128)(2,1)}, u32[]{:S(2)}) copy-start(bf16[512,128]{0,1:T(8,128)(2,1)} %copy.362) | copy-start | bytes 393220
  212.8 1.4 copy-start.26
  266.7 1.8 copy-start.6
  266.7 2.4 copy-start.2
  266.7 2.4 copy-start.31
  266.7 2.4 copy-start.32
  266.7 2.4 copy-start.48
  268.4 1.2 copy-start.46
  269.1 1.1 copy-start.7
  269.1 1.1 copy-start.8
  269.5 1.4 copy-start.13
  269.6 1.4 copy-start.27
  269.6 1.4 copy-start.30
  271.0 1.2 copy-start.51
  271.0 1.2 copy-start.52
  272.6 1.1 copy-start.40
  272.7 3.4 copy-start.47
  272.7 5.2 copy-start.53
  273.7 62.3 %all-gather.25.cloned.1.call-start = ((), (), s32[]{:S(2)}) async-start(), calls=%async_computation.5 | async-start | bytes 1966080 | tf_op jit(solution)/shard_map/all_gather | solution.py:11
  279.4 3.5 copy-start.39
  280.4 85.0 %all-gather.27.cloned.1.call-start = ((), (), s32[]{:S(2)}) async-start(), calls=%async_computation.6 | async-start | bytes 2359296 | tf_op jit(solution)/shard_map/all_gather | solution.py:11
  280.4 3.2 copy-start.23
  281.3 133.8 %all-gather.17.cloned.1.call-start = ((), (), s32[]{:S(2)}) async-start(), calls=%async_computation.1 | async-start | bytes 2359296 | tf_op jit(solution)/shard_map/all_gather | solution.py:11
  283.7 1.6 copy-start.33
  284.9 2.2 copy-start.15
  284.9 2.2 copy-start.44
  284.9 0.7 copy-start.28
  285.6 26.4 %copy-start.24 = (pred[128,128]{1,0:T(8,128)(4,1)S(1)}, pred[128,128]{1,0:T(8,128)(4,1)}, u32[]{:S(2)}) copy-start(pred[128,128]{1,0:T(8,128)(4,1)} %iota_compare_fusion.1) | copy-start | bytes 49156
  285.6 46.5 %copy-start.45 = (pred[2]{0:T(512)(128)(4,1)S(1)}, pred[2]{0:T(512)(128)(4,1)}, u32[]{:S(2)}) copy-start(pred[2]{0:T(512)(128)(4,1)} %get-tuple-element.155) | copy-start | bytes 10
  332.2 1.4 copy-start.29
  332.2 1.4 copy-start.34
  334.0 84.1 %copy-start.9 = (bf16[3,2,512,128]{2,3,1,0:T(8,128)(2,1)}, bf16[3,2,512,128]{2,3,1,0:T(8,128)(2,1)S(1)}, u32[]{:S(2)}) copy-start(bf16[3,2,512,128]{2,3,1,0:T(8,128)(2,1)S(1)} %fusion.40) | copy-start | bytes 2359300
  418.0 1.1 copy-start.3
  418.1 1.0 copy-start.17
  418.1 1.0 copy-start.37
  420.7 2.8 copy-start.21
  420.7 2.8 copy-start.25
  420.7 2.8 copy-start.35
  555.1 1.5 copy-start.4
  556.7 1.5 copy-start.49
  558.2 1.1 copy-start.10
  558.2 1.4 copy-start.18
Sparse Core Ops, SparseCore 0:
  13.6 22.3 all-gather.22
  38.1 19.6 all-gather.18
  59.9 49.0 all-gather.14
  111.0 47.6 all-gather.20
  273.8 18.1 all-gather.28
  294.0 19.8 all-gather.24
  316.0 49.2 all-gather.26
  367.5 47.6 all-gather.16
